TPU v7x, 256 devices: a whole 4x4x8 slice. The times are simulated.
256 devices in a mesh: gx: 8 (over x, core), gy: 4 (over y), gz: 8 (over z).
Axes of the slice: x: 4, y: 4, z: 8, core: 2. Of those that a mesh axis runs over, the one named last changes fastest.
Arguments:
- left_core: float32 [256, 4096, 256], P(None, ('gx', 'gy', 'gz')), may hold values from -4000 to 4000
- right_core: float32 [256, 4096, 256], P(None, ('gx', 'gy', 'gz')), may hold values from -0.00012207031 to 0.00012207031
Outputs:
- left_out: float32 [256, 4096, 128], P(None, ('gx', 'gy', 'gz'))
- right_out: float32 [128, 4096, 256], P(None, ('gx', 'gy', 'gz'))
- next_factor: float32 [256, 256], replicated
All inputs are finite; a program needn't handle non-finite values.
Results may differ from a plain program's by a relative error of at most 0.000075.
Values sent between devices are 32-bit elements; how exact they have to be, the bound alone decides.
A program may use at most 192 MiB of HBM per device.

v0:
```python
import math
import jax
import jax.numpy as jnp
from jax import lax
from jax.sharding import PartitionSpec as P

RK = 128


def gram_of(matrix_rows):
    return lax.dot_general(
        matrix_rows,
        matrix_rows,
        (((0,), (0,)), ((), ())),
        precision=lax.Precision.HIGHEST,
        preferred_element_type=jnp.float32,
    )


def per_device(left_core, right_core):
    rank_left, points_local, rank_mid = left_core.shape
    rank_right = right_core.shape[2]
    total_points = points_local * lax.axis_size("gx") * lax.axis_size("gy") * lax.axis_size("gz")
    unfold = left_core.reshape(rank_left * points_local, rank_mid)
    lower_one = jnp.linalg.cholesky(lax.psum(gram_of(unfold), ("gx", "gy", "gz")))
    upper_full = lower_one.T
    ortho_cols = lax.linalg.triangular_solve(
        lower_one[:RK, :RK], unfold[:, :RK], left_side=False, lower=True, transpose_a=True
    )
    left_out = (ortho_cols * math.sqrt(rank_left * total_points)).reshape(
        rank_left, points_local, RK
    )
    absorbed = jnp.dot(
        upper_full[:RK, :],
        right_core.reshape(rank_mid, points_local * rank_right),
        precision=lax.Precision.HIGHEST,
        preferred_element_type=jnp.float32,
    )
    summed = lax.psum(gram_of(absorbed.reshape(RK * points_local, rank_right)), ("gx", "gy", "gz"))
    factor = jnp.linalg.cholesky(summed / (RK * total_points)).T
    right_out = absorbed.reshape(RK, points_local, rank_right)
    return (left_out, right_out, factor)


def solution(mesh):
    in_specs = (P(None, ("gx", "gy", "gz"), None), P(None, ("gx", "gy", "gz"), None))
    out_specs = (P(None, ("gx", "gy", "gz"), None), P(None, ("gx", "gy", "gz"), None), P())
    return jax.shard_map(
        per_device, mesh=mesh, in_specs=in_specs, out_specs=out_specs, check_vma=False
    )
```

profile of v0, /device:TPU:2, one launch (start us, length us, event | category | flops | bytes accessed | tf_op | source)
XLA Modules:
  0.0 617.6 jit_solution(7845188268302011180)
XLA Ops:
  7.2 10.9 %convolution_bitcast_fusion = f32[256,256]{0,1:T(8,128)} fusion(f32[256,16,256]{2,1,0:T(8,128)} %param.3), kind=kOutput, calls=%fused_computation.3 | convolution fusion | flops 3221225472 | bytes 4456448 | tf_op jit(solution)/shard_map/dot_general | solution.py:11
  18.6 7.9 %copy.26 = f32[32,8,16,256]{3,1,2,0:T(8,128)} copy(f32[32,8,16,256]{3,2,1,0:T(8,128)} %bitcast.53) | data formatting | bytes 8388608
  26.5 244.9 %all-reduce.4.cloned.1.call-done = f32[256,256]{0,1:T(8,128)} async-done(((f32[256,256]{0,1:T(8,128)}), f32[256,256]{0,1:T(8,128)}) %all-reduce.4.cloned.1.call-update) | async-done | bytes 262160 | tf_op jit(solution)/shard_map/psum | solution.py:25
  271.5 1.1 copy.16
  272.6 1.0 fusion.3
  273.6 11.7 %cholesky.130 = f32[128,128]{1,0:T(8,128)S(1)} custom-call(f32[128,128]{1,0:T(8,128)S(1)} %cholesky.194), custom_call_target="Cholesky" | custom-call | tf_op jit(solution)/shard_map/jit(cholesky)/cholesky | solution.py:25
  285.3 9.8 %custom-call.13 = f32[1,128,128]{1,2,0:T(8,128)S(1)} custom-call(f32[1,128,128]{2,1,0:T(8,128)S(1)} %get-tuple-element.17), custom_call_target="InvertDiagBlocksLowerTriangular" | custom-call | tf_op jit(solution)/shard_map/jit(cholesky)/cholesky | solution.py:25
  295.6 11.9 %cholesky.147 = f32[128,128]{1,0:T(8,128)S(1)} custom-call(f32[128,128]{1,0:T(8,128)S(1)} %convolution_subtract_fusion.1), custom_call_target="Cholesky" | custom-call | tf_op jit(solution)/shard_map/jit(cholesky)/cholesky | solution.py:25
  307.5 0.6 compare_reduce_fusion.2
  309.6 4.5 fusion.4
  314.1 1.5 reshape.39
  315.5 6.4 %fusion.14 = f32[256,256]{0,1:T(8,128)} fusion(f32[2048,256]{1,0:T(8,128)} %reshape.39), kind=kOutput, calls=%fused_computation.41 | convolution fusion | flops 1610612736 | bytes 2359296 | tf_op jit(solution)/shard_map/dot_general | solution.py:11
  322.0 9.8 %custom-call.11 = f32[1,128,128]{1,2,0:T(8,128)S(1)} custom-call(f32[1,128,128]{2,1,0:T(8,128)S(1)} %fusion.8), custom_call_target="InvertDiagBlocksLowerTriangular" | custom-call | tf_op jit(solution)/shard_map/triangular_solve | solution.py:27
  331.8 4.9 fusion
  336.7 2.0 copy.27
  338.6 3.1 copy.17
  341.7 229.4 %all-reduce.6.cloned.1.call-done = f32[256,256]{0,1:T(8,128)} async-done(((f32[256,256]{0,1:T(8,128)}), f32[256,256]{0,1:T(8,128)}) %all-reduce.6.cloned.1.call-update) | async-done | bytes 262160 | tf_op jit(solution)/shard_map/psum | solution.py:39
  571.1 1.0 broadcast_multiply_fusion
  572.2 1.0 fusion.2
  573.2 11.7 %cholesky.164 = f32[128,128]{1,0:T(8,128)S(1)} custom-call(f32[128,128]{1,0:T(8,128)S(1)} %cholesky.197), custom_call_target="Cholesky" | custom-call | tf_op jit(solution)/shard_map/jit(cholesky)/cholesky | solution.py:40
  585.0 9.8 %custom-call.14 = f32[1,128,128]{1,2,0:T(8,128)S(1)} custom-call(f32[1,128,128]{2,1,0:T(8,128)S(1)} %get-tuple-element.13), custom_call_target="InvertDiagBlocksLowerTriangular" | custom-call | tf_op jit(solution)/shard_map/jit(cholesky)/cholesky | solution.py:40
  595.3 11.7 %cholesky.181 = f32[128,128]{1,0:T(8,128)S(1)} custom-call(f32[128,128]{1,0:T(8,128)S(1)} %convolution_subtract_fusion), custom_call_target="Cholesky" | custom-call | tf_op jit(solution)/shard_map/jit(cholesky)/cholesky | solution.py:40
  607.0 0.7 compare_reduce_fusion
  609.7 0.8 copy.20
  (22 shorter events, 2.6 us)
Async XLA Ops:
  7.2 264.3 %all-reduce.4.cloned.1.call-start = ((), (), s32[]{:S(2)}) async-start(), calls=%async_computation | async-start | bytes 524288 | tf_op jit(solution)/shard_map/psum | solution.py:25
  18.1 552.9 %all-reduce.6.cloned.1.call-start = ((), (), s32[]{:S(2)}) async-start(), calls=%async_computation.1 | async-start | bytes 524288 | tf_op jit(solution)/shard_map/psum | solution.py:39
Sparse Core Ops, SparseCore 0:
  18.2 253.1 all-reduce.3
  322.1 248.9 all-reduce.5
where the time goes:
time: 623 us; the launch traced here: 618 us
  waiting for transfers between devices  474 us (76%)
  other arithmetic  81.6 us (13%)
  matrix products  27.6 us (4%)
  between operations  17.1 us (3%)
  local copies, waits for them, and re-layouts  16.5 us (3%)
    psum x1, waiting for transfers between devices, per_device(): lax.psum(gram_of(unfold), ('gx', 'gy', 'gz'))  245 us
    psum x1, waiting for transfers between devices, per_device(): lax.psum(gram_of(absorbed.reshape(RK * points_local, rank_right)), ('gx',...  229 us
    another operation x7, other arithmetic, per_device(): factor = jnp.linalg.cholesky(summed / (RK * total_points)).T  34.7 us
    another operation x6, other arithmetic, per_device(): jnp.linalg.cholesky(lax.psum(gram_of(unfold), ('gx', 'gy', 'gz')))  34.1 us
    dot_general x2, matrix products, gram_of(): lax.dot_general(matrix_rows, matrix_rows, (((0,), (0,)), ((), ())), preci...  17.3 us
  transfers between devices with their start and end apart: 2, of which 2 were waited for; matrix products, arithmetic and copies ran while one was open for 4% of the time, Pallas kernels for 0%

commit v1 on v0

--- a/solution.py
+++ b/solution.py
@@ -36,7 +36,9 @@
         precision=lax.Precision.HIGHEST,
         preferred_element_type=jnp.float32,
     )
-    summed = lax.psum(gram_of(absorbed.reshape(RK * points_local, rank_right)), ("gx", "gy", "gz"))
+    summed = lax.psum(
+        lax.psum(gram_of(absorbed.reshape(RK * points_local, rank_right)), ("gy", "gz")), "gx"
+    )
     factor = jnp.linalg.cholesky(summed / (RK * total_points)).T
     right_out = absorbed.reshape(RK, points_local, rank_right)
     return (left_out, right_out, factor)

time: 623 us -> 581 us (0.933)
  waiting for transfers between devices: 474 us -> 430 us
    psum x1 -> x2, waiting for transfers between devices: 229 us -> 185 us  [the longest x1 133 us: per_device(): lax.psum(gram_of(absorbed.reshape(RK * points_local, rank_right)), ('gy',...]
  transfers between devices with their start and end apart: 2 -> 3, of which waited for: 2 -> 3; matrix products, arithmetic and copies ran while one was open for 4% -> 5% of each run, Pallas kernels for 0% -> 0%
where the time goes in v1:
time: 581 us; the launch traced here: 573 us
  waiting for transfers between devices  430 us (74%)
  other arithmetic  81.6 us (14%)
  matrix products  27.6 us (5%)
  between operations  16.8 us (3%)
  local copies, waits for them, and re-layouts  16.5 us (3%)
    psum x1, waiting for transfers between devices, per_device(): lax.psum(gram_of(unfold), ('gx', 'gy', 'gz'))  245 us
    psum x1, waiting for transfers between devices, per_device(): lax.psum(gram_of(absorbed.reshape(RK * points_local, rank_right)), ('gy',...  133 us
    psum x1, waiting for transfers between devices, per_device(): lax.psum(lax.psum(gram_of(absorbed.reshape(RK * points_local, rank_right)...  52.1 us
    another operation x7, other arithmetic, per_device(): factor = jnp.linalg.cholesky(summed / (RK * total_points)).T  34.7 us
    another operation x6, other arithmetic, per_device(): jnp.linalg.cholesky(lax.psum(gram_of(unfold), ('gx', 'gy', 'gz')))  34.1 us
    dot_general x2, matrix products, gram_of(): lax.dot_general(matrix_rows, matrix_rows, (((0,), (0,)), ((), ())), preci...  17.3 us
  transfers between devices with their start and end apart: 3, of which 3 were waited for; matrix products, arithmetic and copies ran while one was open for 5% of the time, Pallas kernels for 0%

profile of v1, /device:TPU:2, one launch (start us, length us, event | category | flops | bytes accessed | tf_op | source)
XLA Modules:
  0.0 573.3 jit_solution(3086018832396310289)
XLA Ops:
  7.2 10.9 %convolution_bitcast_fusion = f32[256,256]{0,1:T(8,128)} fusion(f32[256,16,256]{2,1,0:T(8,128)} %param.3), kind=kOutput, calls=%fused_computation.3 | convolution fusion | flops 3221225472 | bytes 4456448 | tf_op jit(solution)/shard_map/dot_general | solution.py:11
  18.6 7.9 %copy.26 = f32[32,8,16,256]{3,1,2,0:T(8,128)} copy(f32[32,8,16,256]{3,2,1,0:T(8,128)} %bitcast.53) | data formatting | bytes 8388608
  26.5 244.9 %all-reduce.5.cloned.1.call-done = f32[256,256]{0,1:T(8,128)} async-done(((f32[256,256]{0,1:T(8,128)}), f32[256,256]{0,1:T(8,128)}) %all-reduce.5.cloned.1.call-update) | async-done | bytes 262160 | tf_op jit(solution)/shard_map/psum | solution.py:25
  271.5 1.1 copy.16
  272.6 1.0 fusion.3
  273.6 11.7 %cholesky.130 = f32[128,128]{1,0:T(8,128)S(1)} custom-call(f32[128,128]{1,0:T(8,128)S(1)} %cholesky.194), custom_call_target="Cholesky" | custom-call | tf_op jit(solution)/shard_map/jit(cholesky)/cholesky | solution.py:25
  285.3 9.8 %custom-call.13 = f32[1,128,128]{1,2,0:T(8,128)S(1)} custom-call(f32[1,128,128]{2,1,0:T(8,128)S(1)} %get-tuple-element.17), custom_call_target="InvertDiagBlocksLowerTriangular" | custom-call | tf_op jit(solution)/shard_map/jit(cholesky)/cholesky | solution.py:25
  295.6 11.9 %cholesky.147 = f32[128,128]{1,0:T(8,128)S(1)} custom-call(f32[128,128]{1,0:T(8,128)S(1)} %convolution_subtract_fusion.1), custom_call_target="Cholesky" | custom-call | tf_op jit(solution)/shard_map/jit(cholesky)/cholesky | solution.py:25
  309.5 4.5 fusion.4
  314.0 1.5 reshape.39
  315.5 6.4 %fusion.14 = f32[256,256]{0,1:T(8,128)} fusion(f32[2048,256]{1,0:T(8,128)} %reshape.39), kind=kOutput, calls=%fused_computation.41 | convolution fusion | flops 1610612736 | bytes 2359296 | tf_op jit(solution)/shard_map/dot_general | solution.py:11
  322.0 9.8 %custom-call.11 = f32[1,128,128]{1,2,0:T(8,128)S(1)} custom-call(f32[1,128,128]{2,1,0:T(8,128)S(1)} %fusion.8), custom_call_target="InvertDiagBlocksLowerTriangular" | custom-call | tf_op jit(solution)/shard_map/triangular_solve | solution.py:27
  331.8 133.2 %all-reduce.7.cloned.1.call-done = f32[256,256]{0,1:T(8,128)} async-done(((f32[256,256]{0,1:T(8,128)}), f32[256,256]{0,1:T(8,128)}) %all-reduce.7.cloned.1.call-update) | async-done | bytes 262160 | tf_op jit(solution)/shard_map/psum | solution.py:40
  465.0 4.9 fusion
  469.9 2.0 copy.27
  471.9 3.1 copy.17
  474.9 52.1 %all-reduce.9.cloned.1.call-done = f32[256,256]{0,1:T(8,128)} async-done(((f32[256,256]{0,1:T(8,128)}), f32[256,256]{0,1:T(8,128)}) %all-reduce.9.cloned.1.call-update) | async-done | bytes 262160 | tf_op jit(solution)/shard_map/psum | solution.py:39
  527.0 1.0 broadcast_multiply_fusion
  528.1 1.0 fusion.2
  529.1 11.7 %cholesky.164 = f32[128,128]{1,0:T(8,128)S(1)} custom-call(f32[128,128]{1,0:T(8,128)S(1)} %cholesky.197), custom_call_target="Cholesky" | custom-call | tf_op jit(solution)/shard_map/jit(cholesky)/cholesky | solution.py:42
  540.9 9.8 %custom-call.14 = f32[1,128,128]{1,2,0:T(8,128)S(1)} custom-call(f32[1,128,128]{2,1,0:T(8,128)S(1)} %get-tuple-element.13), custom_call_target="InvertDiagBlocksLowerTriangular" | custom-call | tf_op jit(solution)/shard_map/jit(cholesky)/cholesky | solution.py:42
  551.2 11.7 %cholesky.181 = f32[128,128]{1,0:T(8,128)S(1)} custom-call(f32[128,128]{1,0:T(8,128)S(1)} %convolution_subtract_fusion), custom_call_target="Cholesky" | custom-call | tf_op jit(solution)/shard_map/jit(cholesky)/cholesky | solution.py:42
  563.0 0.7 compare_reduce_fusion
  565.7 0.8 copy.20
  (25 shorter events, 3.3 us)
Async XLA Ops:
  7.2 264.3 %all-reduce.5.cloned.1.call-start = ((), (), s32[]{:S(2)}) async-start(), calls=%async_computation | async-start | bytes 524288 | tf_op jit(solution)/shard_map/psum | solution.py:25
  18.1 446.9 %all-reduce.7.cloned.1.call-start = ((), (), s32[]{:S(2)}) async-start(), calls=%async_computation.1 | async-start | bytes 524288 | tf_op jit(solution)/shard_map/psum | solution.py:40
  321.9 205.1 %all-reduce.9.cloned.1.call-start = ((), (), s32[]{:S(2)}) async-start(), calls=%async_computation.2 | async-start | bytes 524288 | tf_op jit(solution)/shard_map/psum | solution.py:39
Sparse Core Ops, SparseCore 0:
  18.2 253.1 all-reduce.4
  322.0 142.9 all-reduce.6
  467.3 59.6 all-reduce.8
